TPU v7x, 32 devices: a whole 2x2x4 slice. The times are simulated.
32 devices in a mesh: wide: 8 (over z, x), narrow: 4 (over y, core).
Axes of the slice: x: 2, y: 2, z: 4, core: 2. Of those that a mesh axis runs over, the one named last changes fastest.
Arguments:
- samples: bfloat16 [16384, 1024], P(('wide', 'narrow')), may hold values from -16 to 16
- centroid_table: bfloat16 [16384, 1024], P('wide', 'narrow'), may hold values from -6 to 6
- owner: int32 [16384], replicated, may hold values from 0 to 7, as said below
- slot: int32 [16384], replicated, may hold values from 0 to 2047, as said below
- assign: int32 [16384], P('wide'), may hold values from 0 to 16383, as said below
- codebook: float32 [8, 2048, 128], P('narrow'), may hold values from -16 to 16
Outputs:
- residual: bfloat16 [16384, 1024], P('wide', 'narrow')
- refined: float32 [8, 2048, 128], P('narrow')
Inputs may be any that keep to these rules, and one draw needn't show every extreme that they name: owner and slot give each coarse centroid a distinct storage position owner * 2048 + slot. `slot`: see owner. `assign`: in each aligned block of 2048 rows (the rows of one index of wide), at most 512 rows have centroids with one owner, and some owner has exactly 512.
All inputs are finite; a program needn't handle non-finite values.
Results may differ from a plain program's by a relative error of at most 0.0079.
Values may be sent and summed in bfloat16 or wider, within the bound.
No kernel may reach another device: no remote copies, remote signals or barrier semaphores. Data moves between devices by JAX's collectives and lax.ppermute only.
A program may use at most 64 MiB of HBM per device.

v0:
```python
import jax
import jax.numpy as jnp
from jax import lax
from jax.sharding import PartitionSpec as P

ITERS = 2
softness_level = 16.0
prior_weight = 1.0


def score_pass(blocks, narrow_words, codeword_norm_values):
    spaces = narrow_words.shape[0]
    words_count = narrow_words.shape[1]
    sub_width = narrow_words.shape[2]

    def block_step(running, row_block):
        inner_product_rows = jnp.einsum(
            "bms,mks->mbk", row_block, narrow_words, preferred_element_type=jnp.float32
        )
        score_matrix = (
            2.0 * inner_product_rows - codeword_norm_values[:, None, :]
        ) / softness_level
        weights_soft = jax.nn.softmax(score_matrix, axis=2).astype(jnp.bfloat16)
        totals = running[0] + jnp.einsum(
            "mbk,bms->mks", weights_soft, row_block, preferred_element_type=jnp.float32
        )
        return ((totals, running[1] + jnp.sum(weights_soft, axis=1, dtype=jnp.float32)), None)

    start = (
        jnp.zeros((spaces, words_count, sub_width), jnp.float32),
        jnp.zeros((spaces, words_count), jnp.float32),
    )
    (totals, counts), ignored = lax.scan(block_step, start, blocks)
    return (totals, counts)


def on_device(samples, centroid_table, owner, slot, assign, codebook):
    regrouped = lax.all_to_all(samples, "narrow", split_axis=1, concat_axis=0, tiled=True)
    group_rows = regrouped.shape[0]
    owner_of = owner[assign]
    slot_of = slot[assign]
    whole = lax.all_gather(centroid_table, "wide", axis=0, tiled=True)
    centre = jnp.take(whole, owner_of * centroid_table.shape[0] + slot_of, axis=0)
    residual = (regrouped.astype(jnp.float32) - centre.astype(jnp.float32)).astype(jnp.bfloat16)
    spaces = codebook.shape[0]
    sub_width = codebook.shape[2]
    block_size = 512
    blocks = residual.reshape(group_rows // block_size, block_size, spaces, sub_width)
    codewords = codebook
    narrow_words = codebook.astype(jnp.bfloat16)
    codeword_norm_values = jnp.sum(codebook * codebook, axis=2)
    for iteration in range(ITERS):
        narrow_words = codewords.astype(jnp.bfloat16)
        codeword_norm_values = jnp.sum(codewords * codewords, axis=2)
        totals, counts = score_pass(blocks, narrow_words, codeword_norm_values)
        totals, counts = lax.psum((totals, counts), "wide")
        codewords = (totals + prior_weight * codewords) / (counts[:, :, None] + prior_weight)
    return (residual, codewords)


def solution(mesh):
    return jax.shard_map(
        on_device,
        mesh=mesh,
        in_specs=(
            P(("wide", "narrow"), None),
            P("wide", "narrow"),
            P(),
            P(),
            P("wide"),
            P("narrow", None, None),
        ),
        out_specs=(P("wide", "narrow"), P("narrow", None, None)),
        check_vma=False,
    )
```

profile of v0, /device:TPU:0, one launch (start us, length us, event | category | flops | bytes accessed | tf_op | source)
XLA Modules:
  0.0 518.3 jit_solution(10853874548214603583)
XLA Ops:
  14.5 11.8 %gather_fusion.1 = s32[2048]{0:T(1024)S(1)} fusion(s32[16384]{0:T(1024)S(1)} %copy-done, s32[2048]{0:T(1024)S(1)} %fusion.55), kind=kCustom, calls=%fused_computation.1 | custom fusion | bytes 24576 | tf_op jit(solution)/shard_map/gather | solution.py:41
  26.3 11.8 %gather_fusion = s32[2048]{0:T(1024)S(1)} fusion(s32[16384]{0:T(1024)S(1)} %copy-done.2, s32[2048]{0:T(1024)S(1)} %fusion.55), kind=kCustom, calls=%fused_computation | custom fusion | bytes 24576 | tf_op jit(solution)/shard_map/gather | solution.py:40
  44.7 92.6 %all-gather.2.cloned.1.call-done = bf16[16384,256]{1,0:T(8,128)(2,1)} async-done(((bf16[2048,256]{1,0:T(8,128)(2,1)}), bf16[16384,256]{1,0:T(8,128)(2,1)}) %all-gather.2.cloned.1.call-update) | async-done | bytes 8388624 | tf_op jit(solution)/shard_map/all_gather | solution.py:42
  137.4 11.1 %gather_fusion.2 = bf16[2048,256]{1,0:T(8,128)(2,1)S(1)} fusion(bf16[16384,256]{1,0:T(8,128)(2,1)} %all-gather.2.cloned.1.call-done, s32[2048]{0:T(1024)S(1)} %broadcast_clamp_fusion), kind=kCustom, calls=%fused_computation.2 | custom fusion | bytes 2105344 | tf_op jit(solution)/shard_map/jit(_take)/gather | solution.py:43
  158.4 69.5 %while.26 = (s32[]{:T(128)}, f32[2,2048,128]{2,1,0:T(8,128)S(1)}, f32[2,2048]{1,0:T(2,128)S(1)}, bf16[4,512,2,128]{3,1,2,0:T(8,128)(2,1)S(1)}, bf16[2,2048,128]{...) while((s32[]{:T(128)}, f32[2,2048,128]{2,1,0:T(8,128)S(1)}, ...), condition=%wide.region_5.6_spmd.clone, body=%wide.region_1.5_spmd.clone.sunk | while | flops 1093670912 | bytes 31023212 | solution.py:33
  158.4 7.2 %fusion.87 = (f32[2,512]{1,0:T(2,128)S(1)}, f32[2,512,2048]{2,1,0:T(8,128)}) fusion(f32[2,2048]{1,0:T(2,128)S(1)} %get-tuple-element.277, bf16[2,2048,128]{2,1,0:T(8,128)(2,1)} %get-tuple-element.276, bf16[4,512,2,128]{3,1,2,0:T(8,128)(2,1)S(1)} %get-tuple-element.275, s32[]{:T(128)S(6)} %copy.24), kind=kOutput, calls=%fused_computation.70.clone.1 | convolution fusion | flops 547358720 | bytes 9719812 | tf_op jit(solution)/shard_map/while/body/eval_jaxpr/sub | solution.py:23
  165.6 5.5 %convert_reduce_fusion.4 = (f32[2,2048]{1,0:T(2,128)S(1)}, bf16[2,512,2048]{2,1,0:T(8,128)(2,1)}) fusion(f32[2,512,2048]{2,1,0:T(8,128)} %get-tuple-element.242, f32[2,512]{1,0:T(2,128)S(1)} %get-tuple-element.243), kind=kLoop, calls=%fused_computation.4.clone.1 | loop fusion | flops 8384512 | bytes 12603392 | tf_op jit(solution)/shard_map/while/body/eval_jaxpr/reduce_sum | solution.py:27
  175.8 7.2 %fusion.87 = (f32[2,512]{1,0:T(2,128)S(1)}, f32[2,512,2048]{2,1,0:T(8,128)}) fusion(f32[2,2048]{1,0:T(2,128)S(1)} %get-tuple-element.277, bf16[2,2048,128]{2,1,0:T(8,128)(2,1)} %get-tuple-element.276, bf16[4,512,2,128]{3,1,2,0:T(8,128)(2,1)S(1)} %get-tuple-element.275, s32[]{:T(128)S(6)} %copy.24), kind=kOutput, calls=%fused_computation.70.clone.1 | convolution fusion | flops 547358720 | bytes 9719812 | tf_op jit(solution)/shard_map/while/body/eval_jaxpr/sub | solution.py:23
  183.0 5.5 %convert_reduce_fusion.4 = (f32[2,2048]{1,0:T(2,128)S(1)}, bf16[2,512,2048]{2,1,0:T(8,128)(2,1)}) fusion(f32[2,512,2048]{2,1,0:T(8,128)} %get-tuple-element.242, f32[2,512]{1,0:T(2,128)S(1)} %get-tuple-element.243), kind=kLoop, calls=%fused_computation.4.clone.1 | loop fusion | flops 8384512 | bytes 12603392 | tf_op jit(solution)/shard_map/while/body/eval_jaxpr/reduce_sum | solution.py:27
  193.2 7.2 %fusion.87 = (f32[2,512]{1,0:T(2,128)S(1)}, f32[2,512,2048]{2,1,0:T(8,128)}) fusion(f32[2,2048]{1,0:T(2,128)S(1)} %get-tuple-element.277, bf16[2,2048,128]{2,1,0:T(8,128)(2,1)} %get-tuple-element.276, bf16[4,512,2,128]{3,1,2,0:T(8,128)(2,1)S(1)} %get-tuple-element.275, s32[]{:T(128)S(6)} %copy.24), kind=kOutput, calls=%fused_computation.70.clone.1 | convolution fusion | flops 547358720 | bytes 9719812 | tf_op jit(solution)/shard_map/while/body/eval_jaxpr/sub | solution.py:23
  200.3 5.5 %convert_reduce_fusion.4 = (f32[2,2048]{1,0:T(2,128)S(1)}, bf16[2,512,2048]{2,1,0:T(8,128)(2,1)}) fusion(f32[2,512,2048]{2,1,0:T(8,128)} %get-tuple-element.242, f32[2,512]{1,0:T(2,128)S(1)} %get-tuple-element.243), kind=kLoop, calls=%fused_computation.4.clone.1 | loop fusion | flops 8384512 | bytes 12603392 | tf_op jit(solution)/shard_map/while/body/eval_jaxpr/reduce_sum | solution.py:27
  210.6 7.2 %fusion.87 = (f32[2,512]{1,0:T(2,128)S(1)}, f32[2,512,2048]{2,1,0:T(8,128)}) fusion(f32[2,2048]{1,0:T(2,128)S(1)} %get-tuple-element.277, bf16[2,2048,128]{2,1,0:T(8,128)(2,1)} %get-tuple-element.276, bf16[4,512,2,128]{3,1,2,0:T(8,128)(2,1)S(1)} %get-tuple-element.275, s32[]{:T(128)S(6)} %copy.24), kind=kOutput, calls=%fused_computation.70.clone.1 | convolution fusion | flops 547358720 | bytes 9719812 | tf_op jit(solution)/shard_map/while/body/eval_jaxpr/sub | solution.py:23
  217.7 5.5 %convert_reduce_fusion.4 = (f32[2,2048]{1,0:T(2,128)S(1)}, bf16[2,512,2048]{2,1,0:T(8,128)(2,1)}) fusion(f32[2,512,2048]{2,1,0:T(8,128)} %get-tuple-element.242, f32[2,512]{1,0:T(2,128)S(1)} %get-tuple-element.243), kind=kLoop, calls=%fused_computation.4.clone.1 | loop fusion | flops 8384512 | bytes 12603392 | tf_op jit(solution)/shard_map/while/body/eval_jaxpr/reduce_sum | solution.py:27
  229.4 35.4 %psum.29 = f32[2,2048]{1,0:T(2,128)S(1)} all-reduce(f32[2,2048]{1,0:T(2,128)S(1)} %get-tuple-element.69), channel_id=1, replica_groups=mesh['wide'=8,'narrow'=4] {'wide'}, use_global_device_ids=true, to_apply=%region_7.8 | all-reduce | flops 4096 | bytes 32768 | tf_op jit(solution)/shard_map/psum | solution.py:56
  264.8 65.7 %all-reduce.3.cloned.1.call-done = f32[2,2048,128]{2,1,0:T(8,128)} async-done(((f32[2,2048,128]{2,1,0:T(8,128)}), f32[2,2048,128]{2,1,0:T(8,128)}) %all-reduce.3.cloned.1.call-update) | async-done | bytes 2097168 | tf_op jit(solution)/shard_map/psum | solution.py:56
  335.8 69.5 %while.27 = (s32[]{:T(128)}, f32[2,2048,128]{2,1,0:T(8,128)S(1)}, f32[2,2048]{1,0:T(2,128)S(1)}, bf16[4,512,2,128]{3,1,2,0:T(8,128)(2,1)S(1)}, bf16[2,2048,128]{...) while((s32[]{:T(128)}, f32[2,2048,128]{2,1,0:T(8,128)S(1)}, ...), condition=%wide.region_13.14_spmd.clone, body=%wide.region_9.0_spmd.clone.sunk | while | flops 1093670912 | bytes 31023212 | solution.py:33
  335.8 7.1 %fusion.92 = (f32[2,512]{1,0:T(2,128)S(1)}, f32[2,512,2048]{2,1,0:T(8,128)}) fusion(f32[2,2048]{1,0:T(2,128)S(1)} %get-tuple-element.301, bf16[2,2048,128]{2,1,0:T(8,128)(2,1)} %get-tuple-element.300, bf16[4,512,2,128]{3,1,2,0:T(8,128)(2,1)S(1)} %get-tuple-element.299, s32[]{:T(128)S(6)} %copy.34), kind=kOutput, calls=%fused_computation.71.clone.1 | convolution fusion | flops 547358720 | bytes 9719812 | tf_op jit(solution)/shard_map/while/body/eval_jaxpr/sub | solution.py:23
  342.9 5.5 %convert_reduce_fusion.5 = (f32[2,2048]{1,0:T(2,128)S(1)}, bf16[2,512,2048]{2,1,0:T(8,128)(2,1)}) fusion(f32[2,512,2048]{2,1,0:T(8,128)} %get-tuple-element.252, f32[2,512]{1,0:T(2,128)S(1)} %get-tuple-element.253), kind=kLoop, calls=%fused_computation.28.clone.1 | loop fusion | flops 8384512 | bytes 12603392 | tf_op jit(solution)/shard_map/while/body/eval_jaxpr/reduce_sum | solution.py:27
  353.2 7.2 %fusion.92 = (f32[2,512]{1,0:T(2,128)S(1)}, f32[2,512,2048]{2,1,0:T(8,128)}) fusion(f32[2,2048]{1,0:T(2,128)S(1)} %get-tuple-element.301, bf16[2,2048,128]{2,1,0:T(8,128)(2,1)} %get-tuple-element.300, bf16[4,512,2,128]{3,1,2,0:T(8,128)(2,1)S(1)} %get-tuple-element.299, s32[]{:T(128)S(6)} %copy.34), kind=kOutput, calls=%fused_computation.71.clone.1 | convolution fusion | flops 547358720 | bytes 9719812 | tf_op jit(solution)/shard_map/while/body/eval_jaxpr/sub | solution.py:23
  370.5 7.2 %fusion.92 = (f32[2,512]{1,0:T(2,128)S(1)}, f32[2,512,2048]{2,1,0:T(8,128)}) fusion(f32[2,2048]{1,0:T(2,128)S(1)} %get-tuple-element.301, bf16[2,2048,128]{2,1,0:T(8,128)(2,1)} %get-tuple-element.300, bf16[4,512,2,128]{3,1,2,0:T(8,128)(2,1)S(1)} %get-tuple-element.299, s32[]{:T(128)S(6)} %copy.34), kind=kOutput, calls=%fused_computation.71.clone.1 | convolution fusion | flops 547358720 | bytes 9719812 | tf_op jit(solution)/shard_map/while/body/eval_jaxpr/sub | solution.py:23
  377.7 5.5 %convert_reduce_fusion.5 = (f32[2,2048]{1,0:T(2,128)S(1)}, bf16[2,512,2048]{2,1,0:T(8,128)(2,1)}) fusion(f32[2,512,2048]{2,1,0:T(8,128)} %get-tuple-element.252, f32[2,512]{1,0:T(2,128)S(1)} %get-tuple-element.253), kind=kLoop, calls=%fused_computation.28.clone.1 | loop fusion | flops 8384512 | bytes 12603392 | tf_op jit(solution)/shard_map/while/body/eval_jaxpr/reduce_sum | solution.py:27
  387.9 7.2 %fusion.92 = (f32[2,512]{1,0:T(2,128)S(1)}, f32[2,512,2048]{2,1,0:T(8,128)}) fusion(f32[2,2048]{1,0:T(2,128)S(1)} %get-tuple-element.301, bf16[2,2048,128]{2,1,0:T(8,128)(2,1)} %get-tuple-element.300, bf16[4,512,2,128]{3,1,2,0:T(8,128)(2,1)S(1)} %get-tuple-element.299, s32[]{:T(128)S(6)} %copy.34), kind=kOutput, calls=%fused_computation.71.clone.1 | convolution fusion | flops 547358720 | bytes 9719812 | tf_op jit(solution)/shard_map/while/body/eval_jaxpr/sub | solution.py:23
  412.3 36.7 %psum.31 = f32[2,2048]{1,0:T(2,128)S(1)} all-reduce(f32[2,2048]{1,0:T(2,128)S(1)} %get-tuple-element.71), channel_id=1, replica_groups=mesh['wide'=8,'narrow'=4] {'wide'}, use_global_device_ids=true, to_apply=%region_15.16 | all-reduce | flops 4096 | bytes 32768 | tf_op jit(solution)/shard_map/psum | solution.py:56
  449.0 59.9 %all-reduce.5.cloned.1.call-done = f32[2,2048,128]{2,1,0:T(8,128)} async-done(((f32[2,2048,128]{2,1,0:T(8,128)}), f32[2,2048,128]{2,1,0:T(8,128)}) %all-reduce.5.cloned.1.call-update) | async-done | bytes 2097168 | tf_op jit(solution)/shard_map/psum | solution.py:56
  (70 shorter events, 89.0 us)
Async XLA Ops:
  7.2 7.3 %copy-start = (s32[16384]{0:T(1024)S(1)}, s32[16384]{0:T(1024)}, u32[]{:S(2)}) copy-start(s32[16384]{0:T(1024)} %param.13) | copy-start | bytes 196612
  7.2 130.2 %all-gather.2.cloned.1.call-start = ((), (), s32[]{:S(2)}) async-start(), calls=%async_computation.1 | async-start | bytes 9437184 | tf_op jit(solution)/shard_map/all_gather | solution.py:42
  7.9 6.6 %copy-start.9 = (s32[2048]{0:T(1024)S(1)}, s32[2048]{0:T(1024)}, u32[]{:S(2)}) copy-start(s32[2048]{0:T(1024)} %param.14) | copy-start | bytes 24580
  10.2 31.9 %all-to-all-start = ((bf16[512,4,256]{0,2,1:T(8,128)(2,1)}), bf16[512,4,256]{0,2,1:T(8,128)(2,1)S(1)}, u32[]{:S(2)}, u32[]{:S(2)}) async-start(bf16[512,4,256]{0,2,1:T(8,128)(2,1)} %bitcast), calls=%async_computation | async-start | bytes 2097152 | tf_op jit(solution)/shard_map/all_to_all | solution.py:38
  14.5 316.0 %all-reduce.3.cloned.1.call-start = ((), (), s32[]{:S(2)}) async-start(), calls=%async_computation.2 | async-start | bytes 4194304 | tf_op jit(solution)/shard_map/psum | solution.py:56
  14.5 11.8 %copy-start.2 = (s32[16384]{0:T(1024)S(1)}, s32[16384]{0:T(1024)}, u32[]{:S(2)}) copy-start(s32[16384]{0:T(1024)} %param.12) | copy-start | bytes 196612
  148.5 5.1 copy-start.7
  227.9 1.3 copy-start.3
  229.3 279.6 %all-reduce.5.cloned.1.call-start = ((), (), s32[]{:S(2)}) async-start(), calls=%async_computation.3 | async-start | bytes 4194304 | tf_op jit(solution)/shard_map/psum | solution.py:56
  333.3 1.3 copy-start.5
  405.3 1.3 copy-start.4
  406.6 3.0 copy-start.8
  409.6 99.3 %copy-start.6 = (f32[2,2048,128]{2,1,0:T(8,128)S(1)}, f32[2,2048,128]{2,1,0:T(8,128)}, u32[]{:S(2)}) copy-start(f32[2,2048,128]{2,1,0:T(8,128)} %copy-done.5) | copy-start | bytes 6291460
  449.0 62.8 %copy-start.1 = (s32[16384]{0:T(1024)S(1)}, s32[16384]{0:T(1024)}, u32[]{:S(2)}) copy-start(s32[16384]{0:T(1024)} %param.13) | copy-start | bytes 196612
Sparse Core Ops, SparseCore 0:
  10.1 127.1 all-gather.1
  229.4 101.0 all-reduce.2
  406.7 102.1 all-reduce.4
where the time goes:
time: 519 us; the launch traced here: 518 us
  waiting for transfers between devices  219 us (42%)
  matrix products  94.6 us (18%)
  blocking collectives  72.1 us (14%)
  other arithmetic  63.7 us (12%)
  local copies, waits for them, and re-layouts  50.5 us (10%)
  between operations  14 us (3%)
    psum x2, waiting for transfers between devices, on_device(): totals, counts = lax.psum((totals, counts), 'wide')  126 us
    all_gather x1, waiting for transfers between devices, on_device(): whole = lax.all_gather(centroid_table, 'wide', axis=0, tiled=True)  92.6 us
    psum x2, blocking collectives, on_device(): totals, counts = lax.psum((totals, counts), 'wide')  72.1 us
    sub x8, matrix products, block_step(): weights_soft = jax.nn.softmax(score_matrix, axis=2).astype(jnp.bfloat16)  57.2 us
    reduce_sum x8, other arithmetic, block_step(): jnp.sum(weights_soft, axis=1, dtype=jnp.float32)  44.1 us
    dot_general x8, matrix products, block_step(): jnp.einsum('mbk,bms->mks', weights_soft, row_block, preferred_element_typ...  37.4 us
    gather x3, local copies, waits for them, and re-layouts, on_device(): jnp.take(whole, owner_of * centroid_table.shape[0] + slot_of, axis=0)  16.1 us
    gather x1, local copies, waits for them, and re-layouts, on_device(): slot_of = slot[assign]  11.8 us
  transfers between devices with their start and end apart: 4, of which 3 were waited for; matrix products, arithmetic and copies ran while one was open for 7% of the time, Pallas kernels for 0%

commit v1 on v0

--- a/solution.py
+++ b/solution.py
@@ -39,7 +39,14 @@
     group_rows = regrouped.shape[0]
     owner_of = owner[assign]
     slot_of = slot[assign]
-    whole = lax.all_gather(centroid_table, "wide", axis=0, tiled=True)
+    ways = lax.axis_size("wide")
+    pieces = [centroid_table]
+    for far in range(1, ways):
+        pieces.append(
+            lax.ppermute(pieces[far - 1], "wide", [(d, (d - 1) % ways) for d in range(ways)])
+        )
+    line = jnp.concatenate(pieces, axis=0)
+    whole = jnp.roll(line, lax.axis_index("wide") * centroid_table.shape[0], axis=0)
     centre = jnp.take(whole, owner_of * centroid_table.shape[0] + slot_of, axis=0)
     residual = (regrouped.astype(jnp.float32) - centre.astype(jnp.float32)).astype(jnp.bfloat16)
     spaces = codebook.shape[0]

time: 519 us -> 610 us (1.18)
  local copies, waits for them, and re-layouts: 50.5 us -> 87.7 us
  starting transfers between devices: 4.35 us -> 33.8 us
  waiting for transfers between devices: 219 us -> 238 us
    ppermute x0 -> x7, waiting for transfers between devices: none -> 113 us  [on_device(): lax.ppermute(pieces[far - 1], 'wide', [(d, (d - 1) % ways) for d in range...]
    all_gather x1 -> x0, waiting for transfers between devices: 92.6 us -> none  [on_device(): whole = lax.all_gather(centroid_table, 'wide', axis=0, tiled=True)]
    ppermute x0 -> x7, starting transfers between devices: none -> 30.2 us  [on_device(): lax.ppermute(pieces[far - 1], 'wide', [(d, (d - 1) % ways) for d in range...]
    unnamed x22 -> x47, local copies, waits for them, and re-layouts: 7.86 us -> 36.9 us
    dynamic_slice x0 -> x1, local copies, waits for them, and re-layouts: none -> 7.06 us  [on_device(): jnp.roll(line, lax.axis_index('wide') * centroid_table.shape[0], axis=0)]
  transfers between devices with their start and end apart: 4 -> 10, of which waited for: 3 -> 8; matrix products, arithmetic and copies ran while one was open for 7% -> 9% of each run, Pallas kernels for 0% -> 0%
where the time goes in v1:
time: 610 us; the launch traced here: 609 us
  waiting for transfers between devices  238 us (39%)
  matrix products  94.5 us (15%)
  local copies, waits for them, and re-layouts  87.7 us (14%)
  blocking collectives  75.7 us (12%)
  other arithmetic  64.7 us (11%)
  starting transfers between devices  33.8 us (6%)
  between operations  14.3 us (2%)
    psum x2, waiting for transfers between devices, on_device(): totals, counts = lax.psum((totals, counts), 'wide')  125 us
    ppermute x7, waiting for transfers between devices, on_device(): lax.ppermute(pieces[far - 1], 'wide', [(d, (d - 1) % ways) for d in range...  113 us
    psum x2, blocking collectives, on_device(): totals, counts = lax.psum((totals, counts), 'wide')  75.7 us
    sub x8, matrix products, block_step(): weights_soft = jax.nn.softmax(score_matrix, axis=2).astype(jnp.bfloat16)  57.2 us
    reduce_sum x8, other arithmetic, block_step(): jnp.sum(weights_soft, axis=1, dtype=jnp.float32)  44.2 us
    dot_general x8, matrix products, block_step(): jnp.einsum('mbk,bms->mks', weights_soft, row_block, preferred_element_typ...  37.4 us
    unnamed x47, local copies, waits for them, and re-layouts  36.9 us
    ppermute x7, starting transfers between devices, on_device(): lax.ppermute(pieces[far - 1], 'wide', [(d, (d - 1) % ways) for d in range...  30.2 us
  transfers between devices with their start and end apart: 10, of which 8 were waited for; matrix products, arithmetic and copies ran while one was open for 9% of the time, Pallas kernels for 0%

profile of v1, /device:TPU:0, one launch (start us, length us, event | category | flops | bytes accessed | tf_op | source)
XLA Modules:
  0.0 608.7 jit_solution(7848324485223491642)
XLA Ops:
  13.2 22.7 %collective-permute-done = bf16[2048,256]{1,0:T(8,128)(2,1)S(1)} collective-permute-done((bf16[2048,256]{1,0:T(8,128)(2,1)}, bf16[2048,256]{1,0:T(8,128)(2,1)S(1)}, u32[]{:S(2)}, u32[]{:S(2)}) %collective-permute-start) | collective-permute-done | bytes 1048608 | tf_op jit(solution)/shard_map/ppermute | solution.py:46
  42.0 21.6 %collective-permute-done.1 = bf16[2048,256]{1,0:T(8,128)(2,1)S(1)} collective-permute-done((bf16[2048,256]{1,0:T(8,128)(2,1)S(1)}, bf16[2048,256]{1,0:T(8,128)(2,1)S(1)}, u32[]{:S(2)}, u32[]{:S(2)}) %collective-permute-start.1) | collective-permute-done | bytes 1048608 | tf_op jit(solution)/shard_map/ppermute | solution.py:46
  69.8 20.7 %collective-permute-done.2 = bf16[2048,256]{1,0:T(8,128)(2,1)S(1)} collective-permute-done((bf16[2048,256]{1,0:T(8,128)(2,1)S(1)}, bf16[2048,256]{1,0:T(8,128)(2,1)S(1)}, u32[]{:S(2)}, u32[]{:S(2)}) %collective-permute-start.2) | collective-permute-done | bytes 1048608 | tf_op jit(solution)/shard_map/ppermute | solution.py:46
  102.2 11.8 %gather_fusion = s32[2048]{0:T(1024)S(1)} fusion(s32[16384]{0:T(1024)S(1)} %copy-done, s32[2048]{0:T(1024)S(1)} %fusion.55), kind=kCustom, calls=%fused_computation | custom fusion | bytes 24576 | tf_op jit(solution)/shard_map/gather | solution.py:40
  114.0 11.8 %gather_fusion.1 = s32[2048]{0:T(1024)S(1)} fusion(s32[16384]{0:T(1024)S(1)} %copy-done.2, s32[2048]{0:T(1024)S(1)} %fusion.55), kind=kCustom, calls=%fused_computation.1 | custom fusion | bytes 24576 | tf_op jit(solution)/shard_map/gather | solution.py:41
  128.6 23.1 %collective-permute-done.4 = bf16[2048,256]{1,0:T(8,128)(2,1)} collective-permute-done((bf16[2048,256]{1,0:T(8,128)(2,1)}, bf16[2048,256]{1,0:T(8,128)(2,1)}, u32[]{:S(2)}, u32[]{:S(2)}) %collective-permute-start.4) | collective-permute-done | bytes 1048608 | tf_op jit(solution)/shard_map/ppermute | solution.py:46
  163.7 13.5 %collective-permute-done.5 = bf16[2048,256]{1,0:T(8,128)(2,1)} collective-permute-done((bf16[2048,256]{1,0:T(8,128)(2,1)}, bf16[2048,256]{1,0:T(8,128)(2,1)}, u32[]{:S(2)}, u32[]{:S(2)}) %collective-permute-start.5) | collective-permute-done | bytes 1048608 | tf_op jit(solution)/shard_map/ppermute | solution.py:46
  192.6 11.4 %collective-permute-done.6 = bf16[2048,256]{1,0:T(8,128)(2,1)S(1)} collective-permute-done((bf16[2048,256]{1,0:T(8,128)(2,1)}, bf16[2048,256]{1,0:T(8,128)(2,1)S(1)}, u32[]{:S(2)}, u32[]{:S(2)}) %collective-permute-start.6) | collective-permute-done | bytes 1048608 | tf_op jit(solution)/shard_map/ppermute | solution.py:46
  217.2 7.1 %constant_dynamic-slice_fusion = bf16[16384,256]{1,0:T(8,128)(2,1)} fusion(bf16[32768,256]{1,0:T(8,128)(2,1)} %constant_dynamic-update-slice_fusion, s32[]{:T(128)S(6)} %select_n.46), kind=kLoop, calls=%fused_computation.86 | loop fusion | bytes 16777220 | tf_op jit(solution)/shard_map/jit(_roll_dynamic)/dynamic_slice | solution.py:49
  224.2 11.1 %gather_fusion.2 = bf16[2048,256]{1,0:T(8,128)(2,1)S(1)} fusion(bf16[16384,256]{1,0:T(8,128)(2,1)} %constant_dynamic-slice_fusion, s32[2048]{0:T(1024)S(1)} %broadcast_clamp_fusion), kind=kCustom, calls=%fused_computation.2 | custom fusion | bytes 2105344 | tf_op jit(solution)/shard_map/jit(_take)/gather | solution.py:50
  245.2 69.6 %while.26 = (s32[]{:T(128)}, f32[2,2048,128]{2,1,0:T(8,128)S(1)}, f32[2,2048]{1,0:T(2,128)S(1)}, bf16[4,512,2,128]{3,1,2,0:T(8,128)(2,1)S(1)}, bf16[2,2048,128]{...) while((s32[]{:T(128)}, f32[2,2048,128]{2,1,0:T(8,128)S(1)}, ...), condition=%wide.region_5.6_spmd.clone, body=%wide.region_1.5_spmd.clone.sunk | while | flops 1093670912 | bytes 31023204 | solution.py:33
  245.2 7.1 %fusion.87 = (f32[2,512]{1,0:T(2,128)S(1)}, f32[2,512,2048]{2,1,0:T(8,128)}) fusion(f32[2,2048]{1,0:T(2,128)S(1)} %get-tuple-element.277, bf16[2,2048,128]{2,1,0:T(8,128)(2,1)} %get-tuple-element.276, bf16[4,512,2,128]{3,1,2,0:T(8,128)(2,1)S(1)} %get-tuple-element.275, s32[]{:T(128)} %get-tuple-element.264), kind=kOutput, calls=%fused_computation.87.clone.1 | convolution fusion | flops 547358720 | bytes 9719812 | tf_op jit(solution)/shard_map/while/body/eval_jaxpr/sub | solution.py:23
  262.6 7.2 %fusion.87 = (f32[2,512]{1,0:T(2,128)S(1)}, f32[2,512,2048]{2,1,0:T(8,128)}) fusion(f32[2,2048]{1,0:T(2,128)S(1)} %get-tuple-element.277, bf16[2,2048,128]{2,1,0:T(8,128)(2,1)} %get-tuple-element.276, bf16[4,512,2,128]{3,1,2,0:T(8,128)(2,1)S(1)} %get-tuple-element.275, s32[]{:T(128)} %get-tuple-element.264), kind=kOutput, calls=%fused_computation.87.clone.1 | convolution fusion | flops 547358720 | bytes 9719812 | tf_op jit(solution)/shard_map/while/body/eval_jaxpr/sub | solution.py:23
  280.0 7.2 %fusion.87 = (f32[2,512]{1,0:T(2,128)S(1)}, f32[2,512,2048]{2,1,0:T(8,128)}) fusion(f32[2,2048]{1,0:T(2,128)S(1)} %get-tuple-element.277, bf16[2,2048,128]{2,1,0:T(8,128)(2,1)} %get-tuple-element.276, bf16[4,512,2,128]{3,1,2,0:T(8,128)(2,1)S(1)} %get-tuple-element.275, s32[]{:T(128)} %get-tuple-element.264), kind=kOutput, calls=%fused_computation.87.clone.1 | convolution fusion | flops 547358720 | bytes 9719812 | tf_op jit(solution)/shard_map/while/body/eval_jaxpr/sub | solution.py:23
  297.4 7.2 %fusion.87 = (f32[2,512]{1,0:T(2,128)S(1)}, f32[2,512,2048]{2,1,0:T(8,128)}) fusion(f32[2,2048]{1,0:T(2,128)S(1)} %get-tuple-element.277, bf16[2,2048,128]{2,1,0:T(8,128)(2,1)} %get-tuple-element.276, bf16[4,512,2,128]{3,1,2,0:T(8,128)(2,1)S(1)} %get-tuple-element.275, s32[]{:T(128)} %get-tuple-element.264), kind=kOutput, calls=%fused_computation.87.clone.1 | convolution fusion | flops 547358720 | bytes 9719812 | tf_op jit(solution)/shard_map/while/body/eval_jaxpr/sub | solution.py:23
  316.2 39.3 %psum.29 = f32[2,2048]{1,0:T(2,128)S(1)} all-reduce(f32[2,2048]{1,0:T(2,128)S(1)} %get-tuple-element.69), channel_id=1, replica_groups=mesh['wide'=8,'narrow'=4] {'wide'}, use_global_device_ids=true, to_apply=%region_7.8 | all-reduce | flops 4096 | bytes 32768 | tf_op jit(solution)/shard_map/psum | solution.py:63
  355.5 64.9 %all-reduce.3.cloned.1.call-done = f32[2,2048,128]{2,1,0:T(8,128)} async-done(((f32[2,2048,128]{2,1,0:T(8,128)}), f32[2,2048,128]{2,1,0:T(8,128)}) %all-reduce.3.cloned.1.call-update) | async-done | bytes 2097168 | tf_op jit(solution)/shard_map/psum | solution.py:63
  425.7 69.5 %while.27 = (s32[]{:T(128)}, f32[2,2048,128]{2,1,0:T(8,128)S(1)}, f32[2,2048]{1,0:T(2,128)S(1)}, bf16[4,512,2,128]{3,1,2,0:T(8,128)(2,1)S(1)}, bf16[2,2048,128]{...) while((s32[]{:T(128)}, f32[2,2048,128]{2,1,0:T(8,128)S(1)}, ...), condition=%wide.region_13.14_spmd.clone, body=%wide.region_9.13_spmd.clone.sunk | while | flops 1093670912 | bytes 31023204 | solution.py:33
  425.7 7.1 %fusion.92 = (f32[2,512]{1,0:T(2,128)S(1)}, f32[2,512,2048]{2,1,0:T(8,128)}) fusion(f32[2,2048]{1,0:T(2,128)S(1)} %get-tuple-element.301, bf16[2,2048,128]{2,1,0:T(8,128)(2,1)} %get-tuple-element.300, bf16[4,512,2,128]{3,1,2,0:T(8,128)(2,1)S(1)} %get-tuple-element.299, s32[]{:T(128)} %get-tuple-element.288), kind=kOutput, calls=%fused_computation.88.clone.1 | convolution fusion | flops 547358720 | bytes 9719812 | tf_op jit(solution)/shard_map/while/body/eval_jaxpr/sub | solution.py:23
  443.1 7.1 %fusion.92 = (f32[2,512]{1,0:T(2,128)S(1)}, f32[2,512,2048]{2,1,0:T(8,128)}) fusion(f32[2,2048]{1,0:T(2,128)S(1)} %get-tuple-element.301, bf16[2,2048,128]{2,1,0:T(8,128)(2,1)} %get-tuple-element.300, bf16[4,512,2,128]{3,1,2,0:T(8,128)(2,1)S(1)} %get-tuple-element.299, s32[]{:T(128)} %get-tuple-element.288), kind=kOutput, calls=%fused_computation.88.clone.1 | convolution fusion | flops 547358720 | bytes 9719812 | tf_op jit(solution)/shard_map/while/body/eval_jaxpr/sub | solution.py:23
  460.5 7.1 %fusion.92 = (f32[2,512]{1,0:T(2,128)S(1)}, f32[2,512,2048]{2,1,0:T(8,128)}) fusion(f32[2,2048]{1,0:T(2,128)S(1)} %get-tuple-element.301, bf16[2,2048,128]{2,1,0:T(8,128)(2,1)} %get-tuple-element.300, bf16[4,512,2,128]{3,1,2,0:T(8,128)(2,1)S(1)} %get-tuple-element.299, s32[]{:T(128)} %get-tuple-element.288), kind=kOutput, calls=%fused_computation.88.clone.1 | convolution fusion | flops 547358720 | bytes 9719812 | tf_op jit(solution)/shard_map/while/body/eval_jaxpr/sub | solution.py:23
  477.9 7.1 %fusion.92 = (f32[2,512]{1,0:T(2,128)S(1)}, f32[2,512,2048]{2,1,0:T(8,128)}) fusion(f32[2,2048]{1,0:T(2,128)S(1)} %get-tuple-element.301, bf16[2,2048,128]{2,1,0:T(8,128)(2,1)} %get-tuple-element.300, bf16[4,512,2,128]{3,1,2,0:T(8,128)(2,1)S(1)} %get-tuple-element.299, s32[]{:T(128)} %get-tuple-element.288), kind=kOutput, calls=%fused_computation.88.clone.1 | convolution fusion | flops 547358720 | bytes 9719812 | tf_op jit(solution)/shard_map/while/body/eval_jaxpr/sub | solution.py:23
  502.6 36.5 %psum.31 = f32[2,2048]{1,0:T(2,128)S(1)} all-reduce(f32[2,2048]{1,0:T(2,128)S(1)} %get-tuple-element.71), channel_id=1, replica_groups=mesh['wide'=8,'narrow'=4] {'wide'}, use_global_device_ids=true, to_apply=%region_15.16 | all-reduce | flops 4096 | bytes 32768 | tf_op jit(solution)/shard_map/psum | solution.py:63
  539.1 59.9 %all-reduce.5.cloned.1.call-done = f32[2,2048,128]{2,1,0:T(8,128)} async-done(((f32[2,2048,128]{2,1,0:T(8,128)}), f32[2,2048,128]{2,1,0:T(8,128)}) %all-reduce.5.cloned.1.call-update) | async-done | bytes 2097168 | tf_op jit(solution)/shard_map/psum | solution.py:63
  (108 shorter events, 181.8 us)
Async XLA Ops:
  7.2 95.0 %copy-start = (s32[16384]{0:T(1024)S(1)}, s32[16384]{0:T(1024)}, u32[]{:S(2)}) copy-start(s32[16384]{0:T(1024)} %param.12) | copy-start | bytes 196612
  7.2 106.8 %copy-start.2 = (s32[16384]{0:T(1024)S(1)}, s32[16384]{0:T(1024)}, u32[]{:S(2)}) copy-start(s32[16384]{0:T(1024)} %param.13) | copy-start | bytes 196612
  7.2 28.8 %collective-permute-start = (bf16[2048,256]{1,0:T(8,128)(2,1)}, bf16[2048,256]{1,0:T(8,128)(2,1)S(1)}, u32[]{:S(2)}, u32[]{:S(2)}) collective-permute-start(bf16[2048,256]{1,0:T(8,128)(2,1)} %param.11), channel_id=1, source_target_pairs={{0,28},{4,0},{8,4},{12,8},{16,12},{20,16},{24,20},{28,24},{1,29},{... | collective-permute-start | bytes 3145736 | tf_op jit(solution)/shard_map/ppermute | solution.py:46
  36.0 1.0 copy-start.9
  37.0 26.6 %collective-permute-start.1 = (bf16[2048,256]{1,0:T(8,128)(2,1)S(1)}, bf16[2048,256]{1,0:T(8,128)(2,1)S(1)}, u32[]{:S(2)}, u32[]{:S(2)}) collective-permute-start(bf16[2048,256]{1,0:T(8,128)(2,1)S(1)} %collective-permute-done), channel_id=1, source_target_pairs={{0,28},{4,0},{8,4},{12,8},{16,12},{20,16},{24,20},{28,24},{1,29},{... | collective-permute-start | bytes 3145736 | tf_op jit(solution)/shard_map/ppermute | solution.py:46
  64.6 25.9 %collective-permute-start.2 = (bf16[2048,256]{1,0:T(8,128)(2,1)S(1)}, bf16[2048,256]{1,0:T(8,128)(2,1)S(1)}, u32[]{:S(2)}, u32[]{:S(2)}) collective-permute-start(bf16[2048,256]{1,0:T(8,128)(2,1)S(1)} %collective-permute-done.1), channel_id=1, source_target_pairs={{0,28},{4,0},{8,4},{12,8},{16,12},{20,16},{24,20},{28,24},{1,29},{... | collective-permute-start | bytes 3145736 | tf_op jit(solution)/shard_map/ppermute | solution.py:46
  90.5 35.3 %copy-start.13 = (bf16[2048,256]{1,0:T(8,128)(2,1)}, bf16[2048,256]{1,0:T(8,128)(2,1)S(1)}, u32[]{:S(2)}) copy-start(bf16[2048,256]{1,0:T(8,128)(2,1)S(1)} %collective-permute-done.2) | copy-start | bytes 3145732
  90.5 35.3 %collective-permute-start.3 = (bf16[2048,256]{1,0:T(8,128)(2,1)S(1)}, bf16[2048,256]{1,0:T(8,128)(2,1)}, u32[]{:S(2)}, u32[]{:S(2)}) collective-permute-start(bf16[2048,256]{1,0:T(8,128)(2,1)S(1)} %collective-permute-done.2), channel_id=1, source_target_pairs={{0,28},{4,0},{8,4},{12,8},{16,12},{20,16},{24,20},{28,24},{1,29},{... | collective-permute-start | bytes 3145736 | tf_op jit(solution)/shard_map/ppermute | solution.py:46
  97.9 60.7 %all-to-all-start = ((bf16[512,4,256]{0,2,1:T(8,128)(2,1)}), bf16[512,4,256]{0,2,1:T(8,128)(2,1)S(1)}, u32[]{:S(2)}, u32[]{:S(2)}) async-start(bf16[512,4,256]{0,2,1:T(8,128)(2,1)} %bitcast.64), calls=%async_computation | async-start | bytes 2097152 | tf_op jit(solution)/shard_map/all_to_all | solution.py:38
  101.5 318.9 %all-reduce.3.cloned.1.call-start = ((), (), s32[]{:S(2)}) async-start(), calls=%async_computation.1 | async-start | bytes 4194304 | tf_op jit(solution)/shard_map/psum | solution.py:63
  125.8 25.9 %collective-permute-start.4 = (bf16[2048,256]{1,0:T(8,128)(2,1)}, bf16[2048,256]{1,0:T(8,128)(2,1)}, u32[]{:S(2)}, u32[]{:S(2)}) collective-permute-start(bf16[2048,256]{1,0:T(8,128)(2,1)} %collective-permute-done.3), channel_id=1, source_target_pairs={{0,28},{4,0},{8,4},{12,8},{16,12},{20,16},{24,20},{28,24},{1,29},{... | collective-permute-start | bytes 3145736 | tf_op jit(solution)/shard_map/ppermute | solution.py:46
  151.7 25.5 %collective-permute-start.5 = (bf16[2048,256]{1,0:T(8,128)(2,1)}, bf16[2048,256]{1,0:T(8,128)(2,1)}, u32[]{:S(2)}, u32[]{:S(2)}) collective-permute-start(bf16[2048,256]{1,0:T(8,128)(2,1)} %collective-permute-done.4), channel_id=1, source_target_pairs={{0,28},{4,0},{8,4},{12,8},{16,12},{20,16},{24,20},{28,24},{1,29},{... | collective-permute-start | bytes 3145736 | tf_op jit(solution)/shard_map/ppermute | solution.py:46
  158.6 26.0 %copy-start.14 = (bf16[2048,256]{1,0:T(8,128)(2,1)S(1)}, bf16[2048,256]{1,0:T(8,128)(2,1)}, u32[]{:S(2)}) copy-start(bf16[2048,256]{1,0:T(8,128)(2,1)} %copy-done.13) | copy-start | bytes 3145732
  161.3 43.8 %copy-start.8 = (bf16[2048,256]{1,0:T(8,128)(2,1)S(1)}, bf16[2048,256]{1,0:T(8,128)(2,1)}, u32[]{:S(2)}) copy-start(bf16[2048,256]{1,0:T(8,128)(2,1)} %param.11) | copy-start | bytes 3145732
  161.3 44.9 %copy-start.10 = (bf16[2048,256]{1,0:T(8,128)(2,1)S(1)}, bf16[2048,256]{1,0:T(8,128)(2,1)}, u32[]{:S(2)}) copy-start(bf16[2048,256]{1,0:T(8,128)(2,1)} %copy-done.9) | copy-start | bytes 3145732
  163.7 43.5 %copy-start.12 = (bf16[2048,256]{1,0:T(8,128)(2,1)S(1)}, bf16[2048,256]{1,0:T(8,128)(2,1)}, u32[]{:S(2)}) copy-start(bf16[2048,256]{1,0:T(8,128)(2,1)} %copy-done.11) | copy-start | bytes 3145732
  177.2 26.8 %collective-permute-start.6 = (bf16[2048,256]{1,0:T(8,128)(2,1)}, bf16[2048,256]{1,0:T(8,128)(2,1)S(1)}, u32[]{:S(2)}, u32[]{:S(2)}) collective-permute-start(bf16[2048,256]{1,0:T(8,128)(2,1)} %collective-permute-done.5), channel_id=1, source_target_pairs={{0,28},{4,0},{8,4},{12,8},{16,12},{20,16},{24,20},{28,24},{1,29},{... | collective-permute-start | bytes 3145736 | tf_op jit(solution)/shard_map/ppermute | solution.py:46
  235.4 5.0 copy-start.7
  314.8 1.3 copy-start.3
  316.2 282.8 %all-reduce.5.cloned.1.call-start = ((), (), s32[]{:S(2)}) async-start(), calls=%async_computation.2 | async-start | bytes 4194304 | tf_op jit(solution)/shard_map/psum | solution.py:63
  423.3 1.3 copy-start.5
  495.3 1.3 copy-start.4
  495.3 106.6 %copy-start.1 = (s32[16384]{0:T(1024)S(1)}, s32[16384]{0:T(1024)}, u32[]{:S(2)}) copy-start(s32[16384]{0:T(1024)} %param.12) | copy-start | bytes 196612
  496.6 102.3 %copy-start.6 = (f32[2,2048,128]{2,1,0:T(8,128)S(1)}, f32[2,2048,128]{2,1,0:T(8,128)}, u32[]{:S(2)}) copy-start(f32[2,2048,128]{2,1,0:T(8,128)} %copy-done.5) | copy-start | bytes 6291460
  (1 other events, 1.0 us)
Sparse Core Ops, SparseCore 0:
  316.3 104.0 all-reduce.2
  496.7 102.1 all-reduce.4
